TPU v7x, 32 devices: a whole 2x2x4 slice. The times are simulated.
32 devices in a mesh: region: 8 (over y, x, core), tile: 4 (over z).
Axes of the slice: x: 2, y: 2, z: 4, core: 2. Of those that a mesh axis runs over, the one named last changes fastest.
Arguments:
- params: float32 [256, 59, 128], P(('region', 'tile')), may hold values from -6 to 6
- first_moment: float32 [256, 59, 128], P(('region', 'tile')), may hold values from -0.006 to 0.006
- second_moment: float32 [256, 59, 128], P(('region', 'tile')), may hold values from 1e-09 to 2e-05
- view_basis: float32 [16], replicated, may hold values from -1.5 to 1.5
- target: float32 [32, 3, 1024], P(('region', 'tile')), may hold values from 0 to 1
- tile_blocks: int32 [32, 4], P(('region', 'tile')), may hold values from 0 to 31, as said below
- moving: int32 [32, 4], P(('region', 'tile')), may hold values from 0 to 7, as said below
Outputs:
- new_params: float32 [256, 59, 128], P(('region', 'tile'))
- new_first: float32 [256, 59, 128], P(('region', 'tile'))
- new_second: float32 [256, 59, 128], P(('region', 'tile'))
- image: float32 [32, 3, 1024], P(('region', 'tile'))
Inputs may be any that keep to these rules, and one draw needn't show every extreme that they name: `tile_blocks`: row i lists the blocks of the tile of device i front to back, as ids within that device's region; it names exactly one block of each of the region's 4 devices, the device at tile index k owning ids k * 8 to (k + 1) * 8 - 1. `moving`: row i names 4 different blocks of device i, counted from 0 within the device.
All inputs are finite; a program needn't handle non-finite values.
Results may differ from a plain program's by a relative error of at most 0.0003.
Values sent between devices are 32-bit elements; how exact they have to be, the bound alone decides.
No kernel may reach another device: no remote copies, remote signals or barrier semaphores. Data moves between devices by JAX's collectives and lax.ppermute only.
A program may use at most 64 MiB of HBM per device.

v0:
```python
import jax
import jax.numpy as jnp
from jax import lax
from jax.sharding import PartitionSpec as P

SH = 16
TILE_SIDE = 32
PIX = 1024
beta_one = 0.9
beta_two = 0.999
adam_eps = 1e-08
adam_step = 10.0
highest = lax.Precision.HIGHEST


def shifted(shard, axis, by):
    peers = lax.axis_size(axis)
    return lax.ppermute(shard, axis, [(i, (i + by) % peers) for i in range(peers)])


def step_rates():
    return jnp.concatenate(
        [
            jnp.full((3,), 0.002, jnp.float32),
            jnp.full((3,), 0.005, jnp.float32),
            jnp.full((4,), 0.001, jnp.float32),
            jnp.full((1,), 0.05, jnp.float32),
            jnp.full((3 * SH,), 0.0025, jnp.float32),
        ]
    )


def project(values, view_basis):
    side = float(TILE_SIDE)
    mean_x = 0.5 * side + 0.375 * side * jnp.tanh(values[..., 0, :])
    mean_y = 0.5 * side + 0.375 * side * jnp.tanh(values[..., 1, :])
    zoom_factor = 3.0 / (1.0 + jax.nn.softplus(values[..., 2, :]))
    extent = side / 32.0 * 1.5 * jnp.exp(jnp.tanh(values[..., 3:6, :]))
    extent_sq = extent * extent
    rotation = values[..., 6:10, :]
    rot_norm = jnp.sqrt(jnp.sum(rotation * rotation, axis=-2, keepdims=True))
    rotation = rotation / jnp.maximum(rot_norm, 1.0)
    quat_w = rotation[..., 0, :]
    quat_x = rotation[..., 1, :]
    quat_y = rotation[..., 2, :]
    quat_z = rotation[..., 3, :]
    upper_row = [
        1.0 - 2.0 * (quat_y * quat_y + quat_z * quat_z),
        2.0 * (quat_x * quat_y - quat_w * quat_z),
        2.0 * (quat_x * quat_z + quat_w * quat_y),
    ]
    lower_row = [
        2.0 * (quat_x * quat_y + quat_w * quat_z),
        1.0 - 2.0 * (quat_x * quat_x + quat_z * quat_z),
        2.0 * (quat_y * quat_z - quat_w * quat_x),
    ]
    zoom_sq = zoom_factor * zoom_factor
    cov_xx = (
        zoom_sq
        * (
            upper_row[0] * upper_row[0] * extent_sq[..., 0, :]
            + upper_row[1] * upper_row[1] * extent_sq[..., 1, :]
            + upper_row[2] * upper_row[2] * extent_sq[..., 2, :]
        )
        + 0.3
    )
    cov_yy = (
        zoom_sq
        * (
            lower_row[0] * lower_row[0] * extent_sq[..., 0, :]
            + lower_row[1] * lower_row[1] * extent_sq[..., 1, :]
            + lower_row[2] * lower_row[2] * extent_sq[..., 2, :]
        )
        + 0.3
    )
    cov_xy = zoom_sq * (
        upper_row[0] * lower_row[0] * extent_sq[..., 0, :]
        + upper_row[1] * lower_row[1] * extent_sq[..., 1, :]
        + upper_row[2] * lower_row[2] * extent_sq[..., 2, :]
    )
    determinant = cov_xx * cov_yy - cov_xy * cov_xy
    opacity = 0.99 * jax.nn.sigmoid(values[..., 10, :] - 4.0)
    harmonics = values[..., 11:, :].reshape(values.shape[:-2] + (3, SH, values.shape[-1]))
    colours = jax.nn.sigmoid(
        jnp.einsum("...ckg,k->...cg", harmonics, view_basis, precision=highest)
    )
    return jnp.stack(
        [
            mean_x,
            mean_y,
            cov_yy / determinant,
            -cov_xy / determinant,
            cov_xx / determinant,
            opacity,
            colours[..., 0, :],
            colours[..., 1, :],
            colours[..., 2, :],
        ],
        axis=-2,
    )


def composite(splat_list, wanted):
    width = splat_list.shape[2]
    pixels = jnp.arange(PIX)
    centre_x = (pixels % TILE_SIDE).astype(jnp.float32) + 0.5
    centre_y = (pixels // TILE_SIDE).astype(jnp.float32) + 0.5
    strict = (jnp.arange(width)[:, None] < jnp.arange(width)[None, :]).astype(jnp.float32)
    inclusive_mask = (jnp.arange(width)[:, None] <= jnp.arange(width)[None, :]).astype(jnp.float32)

    def footprint(splats):
        offset_x = centre_x[:, None] - splats[0][None, :]
        offset_y = centre_y[:, None] - splats[1][None, :]
        exponent = -0.5 * (
            splats[2] * offset_x * offset_x
            + 2.0 * splats[3] * offset_x * offset_y
            + splats[4] * offset_y * offset_y
        )
        spread = jnp.exp(exponent)
        alphas = splats[5] * spread
        log_keep = jnp.log1p(-alphas)
        return (offset_x, offset_y, spread, alphas, log_keep)

    def forward(running, splats):
        log_trans, colour_sum = running
        offset_x, offset_y, spread, alphas, log_keep = footprint(splats)
        log_here = log_trans[:, None] + jnp.dot(log_keep, strict, precision=highest)
        weight = alphas * jnp.exp(log_here)
        colour_sum = colour_sum + jnp.dot(weight, splats[6:9].T, precision=highest)
        return ((log_trans + jnp.sum(log_keep, axis=1), colour_sum), None)

    initial = (jnp.zeros((PIX,), jnp.float32), jnp.zeros((PIX, 3), jnp.float32))
    (_, colour_sum), _ = lax.scan(forward, initial, splat_list)
    errors = 2.0 * (colour_sum - wanted.T)
    totals = jnp.sum(errors * colour_sum, axis=1)

    def backward(running, splats):
        log_trans, before = running
        offset_x, offset_y, spread, alphas, log_keep = footprint(splats)
        log_here = log_trans[:, None] + jnp.dot(log_keep, strict, precision=highest)
        trans = jnp.exp(log_here)
        weight = alphas * trans
        shading = jnp.dot(errors, splats[6:9], precision=highest)
        covered = before[:, None] + jnp.dot(weight * shading, inclusive_mask, precision=highest)
        d_alpha = trans * shading - (totals[:, None] - covered) / (1.0 - alphas)
        d_exponent = d_alpha * alphas
        d_colour = jnp.dot(errors.T, weight, precision=highest)
        gradient = jnp.stack(
            [
                jnp.sum(d_exponent * (splats[2] * offset_x + splats[3] * offset_y), axis=0),
                jnp.sum(d_exponent * (splats[3] * offset_x + splats[4] * offset_y), axis=0),
                jnp.sum(-0.5 * offset_x * offset_x * d_exponent, axis=0),
                jnp.sum(-offset_x * offset_y * d_exponent, axis=0),
                jnp.sum(-0.5 * offset_y * offset_y * d_exponent, axis=0),
                jnp.sum(d_alpha * spread, axis=0),
                d_colour[0],
                d_colour[1],
                d_colour[2],
            ]
        )
        return ((log_trans + jnp.sum(log_keep, axis=1), covered[:, -1]), gradient)

    _, splat_grads = lax.scan(
        backward, (jnp.zeros((PIX,), jnp.float32), jnp.zeros((PIX,), jnp.float32)), splat_list
    )
    return (colour_sum.T, splat_grads)


def on_device(params, first_moment, second_moment, view_basis, target, tile_blocks, moving):
    per_device = params.shape[0]
    projected = project(params, view_basis)
    listed = tile_blocks[0]
    region_blocks = lax.all_gather(projected, "tile", axis=0, tiled=True)
    splat_list = jnp.take(region_blocks, listed, axis=0)
    picture, splat_grads = composite(splat_list, target[0])
    region_count = lax.axis_size("tile") * per_device
    onehot = (listed[:, None] == jnp.arange(region_count)[None, :]).astype(jnp.float32)
    dense_grads = jnp.einsum("lr,lkg->rkg", onehot, splat_grads, precision=highest)
    proj_grads = lax.psum_scatter(dense_grads, "tile", scatter_dimension=0, tiled=True)
    _, pullback = jax.vjp(lambda values: project(values, view_basis), params)
    gradient = pullback(proj_grads)[0]
    rates = step_rates()[:, None]
    moment_one = beta_one * first_moment + (1.0 - beta_one) * gradient
    moment_two = beta_two * second_moment + (1.0 - beta_two) * gradient * gradient
    stepped = params - rates * (moment_one / (1.0 - beta_one**adam_step)) / (
        jnp.sqrt(moment_two / (1.0 - beta_two**adam_step)) + adam_eps
    )
    leaving_ids = moving[0]
    incoming = shifted(
        (
            jnp.take(stepped, leaving_ids, axis=0),
            jnp.take(moment_one, leaving_ids, axis=0),
            jnp.take(moment_two, leaving_ids, axis=0),
        ),
        "region",
        1,
    )
    new_params = stepped.at[leaving_ids].set(incoming[0])
    new_first = moment_one.at[leaving_ids].set(incoming[1])
    new_second = moment_two.at[leaving_ids].set(incoming[2])
    return (new_params, new_first, new_second, picture[None])


def solution(mesh):
    in_specs = (
        P(("region", "tile"), None, None),
        P(("region", "tile"), None, None),
        P(("region", "tile"), None, None),
        P(),
        P(("region", "tile"), None, None),
        P(("region", "tile"), None),
        P(("region", "tile"), None),
    )
    out_specs = (
        P(("region", "tile"), None, None),
        P(("region", "tile"), None, None),
        P(("region", "tile"), None, None),
        P(("region", "tile"), None, None),
    )
    return jax.shard_map(
        on_device, mesh=mesh, in_specs=in_specs, out_specs=out_specs, check_vma=False
    )
```

profile of v0, /device:TPU:0, one launch (start us, length us, event | category | flops | bytes accessed | tf_op | source)
XLA Modules:
  0.0 99.5 jit_solution(8393477302530917290)
XLA Ops:
  7.2 0.8 multiply_reduce_fusion.3
  8.0 0.7 multiply_multiply_fusion.6
  10.3 0.7 slice-done
  11.3 15.2 %all_gather.3 = f32[32,9,128]{2,0,1:T(8,128)S(1)} all-gather(f32[8,9,128]{2,0,1:T(8,128)S(1)} %constant_dynamic-update-slice_fusion), channel_id=1, replica_groups=mesh['region'=8,'tile'=4] {'tile'}, dimensions={0}, use_global_device_ids=true | all-gather | bytes 184320 | tf_op jit(solution)/shard_map/all_gather | solution.py:173
  27.2 9.0 %while.28 = (s32[]{:T(128)}, f32[1024]{0:T(1024)S(1)}, f32[1024,3]{0,1:T(4,128)S(1)}, f32[4,9,128]{2,1,0:T(8,128)S(1)}, s32[]{:T(128)}, /*index=5*/s32[]{:T(128)}, s32[]{}, s32[]{}, s32[]{}, s32[]{}, /*index=10*/s32[]{}, s32[]{}) while((s32[]{:T(128)}, f32[1024]{0:T(1024)S(1)}, f32[1024,3]{0,1:T(4,128)S(1)}, ...), condition=%wide.region_3.4_spmd.clone, body=%wide.region_1.3_spmd.clone.sunk | while | flops 211475584 | bytes 1140968 | solution.py:133
  27.8 1.1 %fusion.161 = f32[1024,128]{1,0:T(8,128)S(1)} fusion(f32[1024]{0:T(1024)S(1)} %get-tuple-element.376, f32[128]{0:T(128)S(1)} %get-tuple-element.367, f32[128]{0:T(128)S(1)} %get-tuple-element.368, f32[1024]{0:T(1024)S(1)} %get-tuple-element.369, f32[128]{0:T(128)S(1)} %get-tuple-element.370, f32[128]{0:T(128)S(1)} %get-tuple-element.371, ...), kind=kOutput, calls=%fused_computation.16.clone.1 | convolution fusion | flops 204898304 | bytes 539648 | tf_op jit(solution)/shard_map/while/body/eval_jaxpr/dot_general | solution.py:127
  30.1 1.1 %fusion.161 = f32[1024,128]{1,0:T(8,128)S(1)} fusion(f32[1024]{0:T(1024)S(1)} %get-tuple-element.376, f32[128]{0:T(128)S(1)} %get-tuple-element.367, f32[128]{0:T(128)S(1)} %get-tuple-element.368, f32[1024]{0:T(1024)S(1)} %get-tuple-element.369, f32[128]{0:T(128)S(1)} %get-tuple-element.370, f32[128]{0:T(128)S(1)} %get-tuple-element.371, ...), kind=kOutput, calls=%fused_computation.16.clone.1 | convolution fusion | flops 204898304 | bytes 539648 | tf_op jit(solution)/shard_map/while/body/eval_jaxpr/dot_general | solution.py:127
  32.3 1.1 %fusion.161 = f32[1024,128]{1,0:T(8,128)S(1)} fusion(f32[1024]{0:T(1024)S(1)} %get-tuple-element.376, f32[128]{0:T(128)S(1)} %get-tuple-element.367, f32[128]{0:T(128)S(1)} %get-tuple-element.368, f32[1024]{0:T(1024)S(1)} %get-tuple-element.369, f32[128]{0:T(128)S(1)} %get-tuple-element.370, f32[128]{0:T(128)S(1)} %get-tuple-element.371, ...), kind=kOutput, calls=%fused_computation.16.clone.1 | convolution fusion | flops 204898304 | bytes 539648 | tf_op jit(solution)/shard_map/while/body/eval_jaxpr/dot_general | solution.py:127
  34.6 1.1 %fusion.161 = f32[1024,128]{1,0:T(8,128)S(1)} fusion(f32[1024]{0:T(1024)S(1)} %get-tuple-element.376, f32[128]{0:T(128)S(1)} %get-tuple-element.367, f32[128]{0:T(128)S(1)} %get-tuple-element.368, f32[1024]{0:T(1024)S(1)} %get-tuple-element.369, f32[128]{0:T(128)S(1)} %get-tuple-element.370, f32[128]{0:T(128)S(1)} %get-tuple-element.371, ...), kind=kOutput, calls=%fused_computation.16.clone.1 | convolution fusion | flops 204898304 | bytes 539648 | tf_op jit(solution)/shard_map/while/body/eval_jaxpr/dot_general | solution.py:127
  36.3 20.6 %while.29 = (s32[]{:T(128)}, f32[1024]{0:T(1024)S(1)}, f32[1024]{0:T(1024)S(1)}, f32[4,9,128]{2,0,1:T(4,128)S(1)}, f32[4,9,128]{2,1,0:T(8,128)S(1)}, /*index=5*/...) while((s32[]{:T(128)}, f32[1024]{0:T(1024)S(1)}, ...), condition=%wide.region_13.14_spmd.clone, body=%wide.region_5.13_spmd.clone.sunk | while | flops 423183744 | bytes 3303176 | solution.py:163
  36.4 1.0 fusion.167
  37.3 1.0 %convolution_bitcast_fusion.4 = f32[1024,128]{1,0:T(8,128)S(1)} fusion(f32[1024,3]{0,1:T(4,128)S(1)} %get-tuple-element.472, f32[4,9,128]{2,1,0:T(8,128)S(1)} %get-tuple-element.471, s32[]{:T(128)} %get-tuple-element.452, s32[]{:T(128)S(6)} %add.964), kind=kOutput, calls=%fused_computation.79.clone.1 | convolution fusion | flops 4718592 | bytes 542728 | tf_op jit(solution)/shard_map/while/body/eval_jaxpr/dot_general | solution.py:143
  38.3 1.8 %fusion.168 = (f32[128]{0:T(128)S(1)}, f32[128]{0:T(128)S(1)}, f32[128]{0:T(128)S(1)}, f32[128]{0:T(128)S(1)}, f32[128]{0:T(128)S(1)}, /*index=5*/f32[128]{0:T(128)S(1)}, f32[1024]{0:T(1024)S(1)}, f32[1024,128]{1,0:T(8,128)S(1)}) fusion(f32[128]{0:T(128)S(1)} %get-tuple-element.384, f32[1024]{0:T(1024)S(1)} %get-tuple-element.385, ...), kind=kOutput, calls=%fused_computation.98.clone.1 | convolution fusion | flops 208828672 | bytes 1600000 | tf_op jit(solution)/shard_map/while/body/eval_jaxpr/dot_general | solution.py:144
  40.1 0.7 convolution_bitcast_fusion.5
  41.5 1.0 fusion.167
  42.5 1.0 %convolution_bitcast_fusion.4 = f32[1024,128]{1,0:T(8,128)S(1)} fusion(f32[1024,3]{0,1:T(4,128)S(1)} %get-tuple-element.472, f32[4,9,128]{2,1,0:T(8,128)S(1)} %get-tuple-element.471, s32[]{:T(128)} %get-tuple-element.452, s32[]{:T(128)S(6)} %add.964), kind=kOutput, calls=%fused_computation.79.clone.1 | convolution fusion | flops 4718592 | bytes 542728 | tf_op jit(solution)/shard_map/while/body/eval_jaxpr/dot_general | solution.py:143
  43.5 1.8 %fusion.168 = (f32[128]{0:T(128)S(1)}, f32[128]{0:T(128)S(1)}, f32[128]{0:T(128)S(1)}, f32[128]{0:T(128)S(1)}, f32[128]{0:T(128)S(1)}, /*index=5*/f32[128]{0:T(128)S(1)}, f32[1024]{0:T(1024)S(1)}, f32[1024,128]{1,0:T(8,128)S(1)}) fusion(f32[128]{0:T(128)S(1)} %get-tuple-element.384, f32[1024]{0:T(1024)S(1)} %get-tuple-element.385, ...), kind=kOutput, calls=%fused_computation.98.clone.1 | convolution fusion | flops 208828672 | bytes 1600000 | tf_op jit(solution)/shard_map/while/body/eval_jaxpr/dot_general | solution.py:144
  45.3 0.7 convolution_bitcast_fusion.5
  46.6 1.0 fusion.167
  47.6 1.0 %convolution_bitcast_fusion.4 = f32[1024,128]{1,0:T(8,128)S(1)} fusion(f32[1024,3]{0,1:T(4,128)S(1)} %get-tuple-element.472, f32[4,9,128]{2,1,0:T(8,128)S(1)} %get-tuple-element.471, s32[]{:T(128)} %get-tuple-element.452, s32[]{:T(128)S(6)} %add.964), kind=kOutput, calls=%fused_computation.79.clone.1 | convolution fusion | flops 4718592 | bytes 542728 | tf_op jit(solution)/shard_map/while/body/eval_jaxpr/dot_general | solution.py:143
  48.6 1.8 %fusion.168 = (f32[128]{0:T(128)S(1)}, f32[128]{0:T(128)S(1)}, f32[128]{0:T(128)S(1)}, f32[128]{0:T(128)S(1)}, f32[128]{0:T(128)S(1)}, /*index=5*/f32[128]{0:T(128)S(1)}, f32[1024]{0:T(1024)S(1)}, f32[1024,128]{1,0:T(8,128)S(1)}) fusion(f32[128]{0:T(128)S(1)} %get-tuple-element.384, f32[1024]{0:T(1024)S(1)} %get-tuple-element.385, ...), kind=kOutput, calls=%fused_computation.98.clone.1 | convolution fusion | flops 208828672 | bytes 1600000 | tf_op jit(solution)/shard_map/while/body/eval_jaxpr/dot_general | solution.py:144
  51.8 1.0 fusion.167
  52.8 1.0 %convolution_bitcast_fusion.4 = f32[1024,128]{1,0:T(8,128)S(1)} fusion(f32[1024,3]{0,1:T(4,128)S(1)} %get-tuple-element.472, f32[4,9,128]{2,1,0:T(8,128)S(1)} %get-tuple-element.471, s32[]{:T(128)} %get-tuple-element.452, s32[]{:T(128)S(6)} %add.964), kind=kOutput, calls=%fused_computation.79.clone.1 | convolution fusion | flops 4718592 | bytes 542728 | tf_op jit(solution)/shard_map/while/body/eval_jaxpr/dot_general | solution.py:143
  53.8 1.8 %fusion.168 = (f32[128]{0:T(128)S(1)}, f32[128]{0:T(128)S(1)}, f32[128]{0:T(128)S(1)}, f32[128]{0:T(128)S(1)}, f32[128]{0:T(128)S(1)}, /*index=5*/f32[128]{0:T(128)S(1)}, f32[1024]{0:T(1024)S(1)}, f32[1024,128]{1,0:T(8,128)S(1)}) fusion(f32[128]{0:T(128)S(1)} %get-tuple-element.384, f32[1024]{0:T(1024)S(1)} %get-tuple-element.385, ...), kind=kOutput, calls=%fused_computation.98.clone.1 | convolution fusion | flops 208828672 | bytes 1600000 | tf_op jit(solution)/shard_map/while/body/eval_jaxpr/dot_general | solution.py:144
  56.9 1.0 %fusion.122 = f32[32,9,128]{2,0,1:T(8,128)} fusion(f32[4,9,128]{2,0,1:T(4,128)S(1)} %get-tuple-element.100, s32[4]{0:T(128)S(1)} %bitcast.135), kind=kOutput, calls=%fused_computation.272 | convolution fusion | flops 1769600 | bytes 165904 | tf_op jit(solution)/shard_map/lr,lkg->rkg/dot_general | solution.py:178
  59.1 19.5 %reduce-scatter.2.cloned.1.call-done = f32[8,9,128]{2,0,1:T(8,128)} async-done(((f32[32,9,128]{2,0,1:T(8,128)}), f32[8,9,128]{2,0,1:T(8,128)}) %reduce-scatter.2.cloned.1.call-update) | async-done | bytes 36880 | tf_op jit(solution)/shard_map/reduce_scatter | solution.py:179
  78.7 0.8 fusion.133
  82.9 1.6 %collective-permute-start.1 = (f32[4,59,128]{2,1,0:T(8,128)S(1)}, f32[4,59,128]{2,1,0:T(8,128)S(1)}, u32[]{:S(2)}, u32[]{:S(2)}) collective-permute-start(f32[4,59,128]{2,1,0:T(8,128)S(1)} %get-tuple-element.274), channel_id=1, source_target_pairs={{0,4},{4,8},{8,12},{12,16},{16,20},{20,24},{24,28},{28,0},{1,5},{5... | collective-permute-start | bytes 362504 | tf_op jit(solution)/shard_map/ppermute | solution.py:18
  84.5 3.6 %collective-permute-done.2 = f32[4,59,128]{2,1,0:T(8,128)S(1)} collective-permute-done((f32[4,59,128]{2,1,0:T(8,128)S(1)}, f32[4,59,128]{2,1,0:T(8,128)S(1)}, u32[]{:S(2)}, u32[]{:S(2)}) %collective-permute-start.2) | collective-permute-done | bytes 120864 | tf_op jit(solution)/shard_map/ppermute | solution.py:18
  88.8 0.8 copy.41
  90.3 0.8 copy.40
  91.8 0.8 copy.39
  (132 shorter events, 17.5 us)
Async XLA Ops:
  7.2 3.0 %copy-start = (f32[8,59,128]{2,0,1:T(8,128)S(1)}, f32[8,59,128]{2,0,1:T(8,128)}, u32[]{:S(2)}) copy-start(f32[8,59,128]{2,0,1:T(8,128)} %param.13) | copy-start | bytes 724996
  7.2 71.5 %reduce-scatter.2.cloned.1.call-start = ((), (), s32[]{:S(2)}) async-start(), calls=%async_computation.1 | async-start | bytes 184320 | tf_op jit(solution)/shard_map/reduce_scatter | solution.py:179
  9.4 0.7 copy-start.6
  10.1 0.9 slice-start
  10.3 0.8 copy-start.5
  27.2 9.0 %copy-start.4 = (f32[1,3,1024]{2,0,1:T(1,128)S(1)}, f32[1,3,1024]{2,0,1:T(1,128)}, u32[]{:S(2)}) copy-start(f32[1,3,1024]{2,0,1:T(1,128)} %param.17) | copy-start | bytes 36868
  57.9 0.7 copy-start.8
  78.7 0.8 copy-start.3
  79.6 0.9 copy-start.1
  79.6 1.1 %copy-start.2 = (f32[8,59,128]{2,0,1:T(8,128)S(1)}, f32[8,59,128]{2,0,1:T(8,128)}, u32[]{:S(2)}) copy-start(f32[8,59,128]{2,0,1:T(8,128)} %param.15) | copy-start | bytes 724996
  79.8 0.8 copy-start.7
  82.8 5.3 %collective-permute-start.2 = (f32[4,59,128]{2,1,0:T(8,128)S(1)}, f32[4,59,128]{2,1,0:T(8,128)S(1)}, u32[]{:S(2)}, u32[]{:S(2)}) collective-permute-start(f32[4,59,128]{2,1,0:T(8,128)S(1)} %get-tuple-element.273), channel_id=1, source_target_pairs={{0,4},{4,8},{8,12},{12,16},{16,20},{20,24},{24,28},{28,0},{1,5},{5... | collective-permute-start | bytes 362504 | tf_op jit(solution)/shard_map/ppermute | solution.py:18
  82.9 6.8 %collective-permute-start.1 = (f32[4,59,128]{2,1,0:T(8,128)S(1)}, f32[4,59,128]{2,1,0:T(8,128)S(1)}, u32[]{:S(2)}, u32[]{:S(2)}) collective-permute-start(f32[4,59,128]{2,1,0:T(8,128)S(1)} %get-tuple-element.274), channel_id=1, source_target_pairs={{0,4},{4,8},{8,12},{12,16},{16,20},{20,24},{24,28},{28,0},{1,5},{5... | collective-permute-start | bytes 362504 | tf_op jit(solution)/shard_map/ppermute | solution.py:18
  84.5 6.7 %collective-permute-start = (f32[4,59,128]{2,1,0:T(8,128)S(1)}, f32[4,59,128]{2,1,0:T(8,128)S(1)}, u32[]{:S(2)}, u32[]{:S(2)}) collective-permute-start(f32[4,59,128]{2,1,0:T(8,128)S(1)} %get-tuple-element.275), channel_id=1, source_target_pairs={{0,4},{4,8},{8,12},{12,16},{16,20},{20,24},{24,28},{28,0},{1,5},{5... | collective-permute-start | bytes 362504 | tf_op jit(solution)/shard_map/ppermute | solution.py:18
Sparse Core Ops, SparseCore 0:
  58.0 20.6 reduce-scatter.1
where the time goes:
time: 99.8 us; the launch traced here: 99.5 us
  matrix products  25.5 us (26%)
  waiting for transfers between devices  23.2 us (23%)
  blocking collectives  15.2 us (15%)
  between operations  14.4 us (14%)
  local copies, waits for them, and re-layouts  12.6 us (13%)
  other arithmetic  6.27 us (6%)
  starting transfers between devices  1.75 us (2%)
    reduce_scatter x1, waiting for transfers between devices, on_device(): lax.psum_scatter(dense_grads, 'tile', scatter_dimension=0, tiled=True)  19.5 us
    all_gather x1, blocking collectives, on_device(): region_blocks = lax.all_gather(projected, 'tile', axis=0, tiled=True)  15.2 us
    dot_general x4, matrix products, backward(): jnp.dot(weight * shading, inclusive_mask, precision=highest)  7.1 us
    unnamed x21, local copies, waits for them, and re-layouts  4.67 us
    dot_general x4, matrix products, forward(): log_here = log_trans[:, None] + jnp.dot(log_keep, strict, precision=highest)  4.21 us
    dot_general x4, matrix products, backward(): shading = jnp.dot(errors, splats[6:9], precision=highest)  4.01 us
    dot_general x4, matrix products, backward(): log_here = log_trans[:, None] + jnp.dot(log_keep, strict, precision=highest)  3.89 us
    ppermute x3, waiting for transfers between devices, shifted(): lax.ppermute(shard, axis, [(i, (i + by) % peers) for i in range(peers)])  3.62 us
  transfers between devices with their start and end apart: 4, of which 2 were waited for; matrix products, arithmetic and copies ran while one was open for 4% of the time, Pallas kernels for 0%

commit v1 on v0

--- a/solution.py
+++ b/solution.py
@@ -1,3 +1,4 @@
+import functools
 import jax
 import jax.numpy as jnp
 from jax import lax
@@ -11,6 +12,23 @@
 adam_eps = 1e-08
 adam_step = 10.0
 highest = lax.Precision.HIGHEST
+
+
+def _measure_units(row_data, across):
+    how_many = jax.lax.psum(1, across)
+    inbox = tuple(((to_i, (to_i + 1) % how_many) for to_i in range(how_many)))
+    all_rows = tuple(((to_i, (to_i - 1) % how_many) for to_i in range(how_many)))
+    far_arr, then = ([row_data], [row_data])
+    for _ in range(how_many // 2):
+        far_arr.append(jax.lax.ppermute(far_arr[-1], across, inbox))
+    for _ in [*range((how_many - 1) // 2)]:
+        then.append(jax.lax.ppermute(then[-1], across, all_rows))
+    carry_in = jnp.concatenate([*far_arr[::-1], *then[1:]], axis=0)
+    z = jax.lax.axis_index(across)
+    return jnp.roll(carry_in, (z - how_many // 2) * row_data.shape[0], axis=0)
+
+
+time_shapes = functools.partial(_measure_units, across="tile")
 
 
 def shifted(shard, axis, by):
@@ -170,7 +188,7 @@
     per_device = params.shape[0]
     projected = project(params, view_basis)
     listed = tile_blocks[0]
-    region_blocks = lax.all_gather(projected, "tile", axis=0, tiled=True)
+    region_blocks = time_shapes(projected)
     splat_list = jnp.take(region_blocks, listed, axis=0)
     picture, splat_grads = composite(splat_list, target[0])
     region_count = lax.axis_size("tile") * per_device

time: 99.8 us -> 94.3 us (0.945)
  blocking collectives: 15.2 us -> 0 us
  starting transfers between devices: 1.75 us -> 6.89 us
  waiting for transfers between devices: 23.2 us -> 27.9 us
    all_gather x1 -> x0, blocking collectives: 15.2 us -> none  [on_device(): region_blocks = lax.all_gather(projected, 'tile', axis=0, tiled=True)]
    ppermute x0 -> x3, waiting for transfers between devices: none -> 6.98 us  [the longest x2 6.98 us: _measure_units(): far_arr.append(jax.lax.ppermute(far_arr[-1], across, inbox))]
    ppermute x0 -> x3, starting transfers between devices: none -> 5.17 us  [the longest x2 3.08 us: _measure_units(): far_arr.append(jax.lax.ppermute(far_arr[-1], across, inbox))]
    reduce_scatter x1, waiting for transfers between devices: 19.5 us -> 17.8 us  [on_device(): lax.psum_scatter(dense_grads, 'tile', scatter_dimension=0, tiled=True)]
    unnamed x21 -> x30, local copies, waits for them, and re-layouts: 4.67 us -> 4.07 us
  transfers between devices with their start and end apart: 4 -> 7, of which waited for: 2 -> 4; matrix products, arithmetic and copies ran while one was open for 4% -> 4% of each run, Pallas kernels for 0% -> 0%
where the time goes in v1:
time: 94.3 us; the launch traced here: 93.9 us
  waiting for transfers between devices  27.9 us (30%)
  matrix products  25.5 us (27%)
  between operations  14.6 us (15%)
  local copies, waits for them, and re-layouts  12.1 us (13%)
  starting transfers between devices  6.89 us (7%)
  other arithmetic  6.35 us (7%)
    reduce_scatter x1, waiting for transfers between devices, on_device(): lax.psum_scatter(dense_grads, 'tile', scatter_dimension=0, tiled=True)  17.8 us
    dot_general x4, matrix products, backward(): jnp.dot(weight * shading, inclusive_mask, precision=highest)  7.07 us
    ppermute x2, waiting for transfers between devices, _measure_units(): far_arr.append(jax.lax.ppermute(far_arr[-1], across, inbox))  6.98 us
    dot_general x4, matrix products, forward(): log_here = log_trans[:, None] + jnp.dot(log_keep, strict, precision=highest)  4.22 us
    unnamed x30, local copies, waits for them, and re-layouts  4.07 us
    dot_general x4, matrix products, backward(): shading = jnp.dot(errors, splats[6:9], precision=highest)  4.01 us
    dot_general x4, matrix products, backward(): log_here = log_trans[:, None] + jnp.dot(log_keep, strict, precision=highest)  3.9 us
    ppermute x2, starting transfers between devices, _measure_units(): far_arr.append(jax.lax.ppermute(far_arr[-1], across, inbox))  3.08 us
  transfers between devices with their start and end apart: 7, of which 4 were waited for; matrix products, arithmetic and copies ran while one was open for 4% of the time, Pallas kernels for 0%

profile of v1, /device:TPU:0, one launch (start us, length us, event | category | flops | bytes accessed | tf_op | source)
XLA Modules:
  0.0 93.9 jit_solution(9626013619740349690)
XLA Ops:
  7.2 0.8 multiply_reduce_fusion.3
  9.6 0.8 slice-done
  10.6 3.1 %collective-permute-start = (f32[8,9,128]{2,0,1:T(8,128)S(1)}, f32[8,9,128]{2,0,1:T(8,128)S(1)}, u32[]{:S(2)}, u32[]{:S(2)}) collective-permute-start(f32[8,9,128]{2,0,1:T(8,128)S(1)} %constant_dynamic-update-slice_fusion), channel_id=1, source_target_pairs={{0,1},{1,2},{2,3},{3,0},{4,5},{5,6},{6,7},{7,4},{8,9},{9,10},{10,1... | collective-permute-start | bytes 110600 | tf_op jit(solution)/shard_map/ppermute | solution.py:23
  13.7 2.1 %collective-permute-start.2 = (f32[8,9,128]{2,0,1:T(8,128)S(1)}, f32[8,9,128]{2,0,1:T(8,128)S(1)}, u32[]{:S(2)}, u32[]{:S(2)}) collective-permute-start(f32[8,9,128]{2,0,1:T(8,128)S(1)} %constant_dynamic-update-slice_fusion), channel_id=1, source_target_pairs={{0,3},{1,0},{2,1},{3,2},{4,7},{5,4},{6,5},{7,6},{8,11},{9,8},{10,9... | collective-permute-start | bytes 110600 | tf_op jit(solution)/shard_map/ppermute | solution.py:25
  16.5 1.3 %collective-permute-done = f32[8,9,128]{2,0,1:T(8,128)S(1)} collective-permute-done((f32[8,9,128]{2,0,1:T(8,128)S(1)}, f32[8,9,128]{2,0,1:T(8,128)S(1)}, u32[]{:S(2)}, u32[]{:S(2)}) %collective-permute-start) | collective-permute-done | bytes 36896 | tf_op jit(solution)/shard_map/ppermute | solution.py:23
  17.9 5.7 %collective-permute-done.1 = f32[8,9,128]{2,0,1:T(8,128)S(1)} collective-permute-done((f32[8,9,128]{2,0,1:T(8,128)S(1)}, f32[8,9,128]{2,0,1:T(8,128)S(1)}, u32[]{:S(2)}, u32[]{:S(2)}) %collective-permute-start.1) | collective-permute-done | bytes 36896 | tf_op jit(solution)/shard_map/ppermute | solution.py:23
  24.6 9.0 %while.28 = (s32[]{:T(128)}, f32[1024]{0:T(1024)S(1)}, f32[1024,3]{0,1:T(4,128)S(1)}, f32[4,9,128]{2,1,0:T(8,128)S(1)}, s32[]{:T(128)}, /*index=5*/s32[]{:T(128)}, s32[]{}, s32[]{}, s32[]{}, s32[]{}, /*index=10*/s32[]{}, s32[]{}) while((s32[]{:T(128)}, f32[1024]{0:T(1024)S(1)}, f32[1024,3]{0,1:T(4,128)S(1)}, ...), condition=%wide.region_3.4_spmd.clone, body=%wide.region_1.3_spmd.clone.sunk | while | flops 211475584 | bytes 1140968 | solution.py:151
  25.2 1.1 %fusion.161 = f32[1024,128]{1,0:T(8,128)S(1)} fusion(f32[1024]{0:T(1024)S(1)} %get-tuple-element.379, f32[128]{0:T(128)S(1)} %get-tuple-element.370, f32[128]{0:T(128)S(1)} %get-tuple-element.371, f32[1024]{0:T(1024)S(1)} %get-tuple-element.372, f32[128]{0:T(128)S(1)} %get-tuple-element.373, f32[128]{0:T(128)S(1)} %get-tuple-element.374, ...), kind=kOutput, calls=%fused_computation.16.clone.1 | convolution fusion | flops 204898304 | bytes 539648 | tf_op jit(solution)/shard_map/while/body/eval_jaxpr/dot_general | solution.py:145
  27.5 1.1 %fusion.161 = f32[1024,128]{1,0:T(8,128)S(1)} fusion(f32[1024]{0:T(1024)S(1)} %get-tuple-element.379, f32[128]{0:T(128)S(1)} %get-tuple-element.370, f32[128]{0:T(128)S(1)} %get-tuple-element.371, f32[1024]{0:T(1024)S(1)} %get-tuple-element.372, f32[128]{0:T(128)S(1)} %get-tuple-element.373, f32[128]{0:T(128)S(1)} %get-tuple-element.374, ...), kind=kOutput, calls=%fused_computation.16.clone.1 | convolution fusion | flops 204898304 | bytes 539648 | tf_op jit(solution)/shard_map/while/body/eval_jaxpr/dot_general | solution.py:145
  29.7 1.1 %fusion.161 = f32[1024,128]{1,0:T(8,128)S(1)} fusion(f32[1024]{0:T(1024)S(1)} %get-tuple-element.379, f32[128]{0:T(128)S(1)} %get-tuple-element.370, f32[128]{0:T(128)S(1)} %get-tuple-element.371, f32[1024]{0:T(1024)S(1)} %get-tuple-element.372, f32[128]{0:T(128)S(1)} %get-tuple-element.373, f32[128]{0:T(128)S(1)} %get-tuple-element.374, ...), kind=kOutput, calls=%fused_computation.16.clone.1 | convolution fusion | flops 204898304 | bytes 539648 | tf_op jit(solution)/shard_map/while/body/eval_jaxpr/dot_general | solution.py:145
  32.0 1.1 %fusion.161 = f32[1024,128]{1,0:T(8,128)S(1)} fusion(f32[1024]{0:T(1024)S(1)} %get-tuple-element.379, f32[128]{0:T(128)S(1)} %get-tuple-element.370, f32[128]{0:T(128)S(1)} %get-tuple-element.371, f32[1024]{0:T(1024)S(1)} %get-tuple-element.372, f32[128]{0:T(128)S(1)} %get-tuple-element.373, f32[128]{0:T(128)S(1)} %get-tuple-element.374, ...), kind=kOutput, calls=%fused_computation.16.clone.1 | convolution fusion | flops 204898304 | bytes 539648 | tf_op jit(solution)/shard_map/while/body/eval_jaxpr/dot_general | solution.py:145
  33.7 20.5 %while.29 = (s32[]{:T(128)}, f32[1024]{0:T(1024)S(1)}, f32[1024]{0:T(1024)S(1)}, f32[4,9,128]{2,0,1:T(4,128)S(1)}, f32[4,9,128]{2,1,0:T(8,128)S(1)}, /*index=5*/...) while((s32[]{:T(128)}, f32[1024]{0:T(1024)S(1)}, ...), condition=%wide.region_13.14_spmd.clone, body=%wide.region_5.13_spmd.clone.sunk | while | flops 423183744 | bytes 3303176 | solution.py:181
  33.8 1.0 %fusion.167 = f32[1024,128]{1,0:T(8,128)S(1)} fusion(f32[1024]{0:T(1024)S(1)} %broadcast_select_fusion.8, f32[128]{0:T(128)S(1)} %get-tuple-element.389, f32[128]{0:T(128)S(1)} %get-tuple-element.387, f32[1024]{0:T(1024)S(1)} %get-tuple-element.388, f32[128]{0:T(128)S(1)} %get-tuple-element.390, f32[128]{0:T(128)S(1)} %get-tuple-element.391, ...), kind=kOutput, calls=%fused_computation.81.clone.1 | convolution fusion | flops 203194368 | bytes 539648 | tf_op jit(solution)/shard_map/while/body/eval_jaxpr/dot_general | solution.py:158
  34.7 1.0 %convolution_bitcast_fusion.4 = f32[1024,128]{1,0:T(8,128)S(1)} fusion(f32[1024,3]{0,1:T(4,128)S(1)} %get-tuple-element.475, f32[4,9,128]{2,1,0:T(8,128)S(1)} %get-tuple-element.474, s32[]{:T(128)} %get-tuple-element.455, s32[]{:T(128)S(6)} %add.997), kind=kOutput, calls=%fused_computation.79.clone.1 | convolution fusion | flops 4718592 | bytes 542728 | tf_op jit(solution)/shard_map/while/body/eval_jaxpr/dot_general | solution.py:161
  35.7 1.8 %fusion.168 = (f32[128]{0:T(128)S(1)}, f32[128]{0:T(128)S(1)}, f32[128]{0:T(128)S(1)}, f32[128]{0:T(128)S(1)}, f32[128]{0:T(128)S(1)}, /*index=5*/f32[128]{0:T(128)S(1)}, f32[1024]{0:T(1024)S(1)}, f32[1024,128]{1,0:T(8,128)S(1)}) fusion(f32[128]{0:T(128)S(1)} %get-tuple-element.387, f32[1024]{0:T(1024)S(1)} %get-tuple-element.388, ...), kind=kOutput, calls=%fused_computation.98.clone.1 | convolution fusion | flops 208828672 | bytes 1600000 | tf_op jit(solution)/shard_map/while/body/eval_jaxpr/dot_general | solution.py:162
  38.9 1.0 %fusion.167 = f32[1024,128]{1,0:T(8,128)S(1)} fusion(f32[1024]{0:T(1024)S(1)} %broadcast_select_fusion.8, f32[128]{0:T(128)S(1)} %get-tuple-element.389, f32[128]{0:T(128)S(1)} %get-tuple-element.387, f32[1024]{0:T(1024)S(1)} %get-tuple-element.388, f32[128]{0:T(128)S(1)} %get-tuple-element.390, f32[128]{0:T(128)S(1)} %get-tuple-element.391, ...), kind=kOutput, calls=%fused_computation.81.clone.1 | convolution fusion | flops 203194368 | bytes 539648 | tf_op jit(solution)/shard_map/while/body/eval_jaxpr/dot_general | solution.py:158
  39.9 1.0 %convolution_bitcast_fusion.4 = f32[1024,128]{1,0:T(8,128)S(1)} fusion(f32[1024,3]{0,1:T(4,128)S(1)} %get-tuple-element.475, f32[4,9,128]{2,1,0:T(8,128)S(1)} %get-tuple-element.474, s32[]{:T(128)} %get-tuple-element.455, s32[]{:T(128)S(6)} %add.997), kind=kOutput, calls=%fused_computation.79.clone.1 | convolution fusion | flops 4718592 | bytes 542728 | tf_op jit(solution)/shard_map/while/body/eval_jaxpr/dot_general | solution.py:161
  40.9 1.8 %fusion.168 = (f32[128]{0:T(128)S(1)}, f32[128]{0:T(128)S(1)}, f32[128]{0:T(128)S(1)}, f32[128]{0:T(128)S(1)}, f32[128]{0:T(128)S(1)}, /*index=5*/f32[128]{0:T(128)S(1)}, f32[1024]{0:T(1024)S(1)}, f32[1024,128]{1,0:T(8,128)S(1)}) fusion(f32[128]{0:T(128)S(1)} %get-tuple-element.387, f32[1024]{0:T(1024)S(1)} %get-tuple-element.388, ...), kind=kOutput, calls=%fused_computation.98.clone.1 | convolution fusion | flops 208828672 | bytes 1600000 | tf_op jit(solution)/shard_map/while/body/eval_jaxpr/dot_general | solution.py:162
  44.0 1.0 %fusion.167 = f32[1024,128]{1,0:T(8,128)S(1)} fusion(f32[1024]{0:T(1024)S(1)} %broadcast_select_fusion.8, f32[128]{0:T(128)S(1)} %get-tuple-element.389, f32[128]{0:T(128)S(1)} %get-tuple-element.387, f32[1024]{0:T(1024)S(1)} %get-tuple-element.388, f32[128]{0:T(128)S(1)} %get-tuple-element.390, f32[128]{0:T(128)S(1)} %get-tuple-element.391, ...), kind=kOutput, calls=%fused_computation.81.clone.1 | convolution fusion | flops 203194368 | bytes 539648 | tf_op jit(solution)/shard_map/while/body/eval_jaxpr/dot_general | solution.py:158
  45.0 1.0 %convolution_bitcast_fusion.4 = f32[1024,128]{1,0:T(8,128)S(1)} fusion(f32[1024,3]{0,1:T(4,128)S(1)} %get-tuple-element.475, f32[4,9,128]{2,1,0:T(8,128)S(1)} %get-tuple-element.474, s32[]{:T(128)} %get-tuple-element.455, s32[]{:T(128)S(6)} %add.997), kind=kOutput, calls=%fused_computation.79.clone.1 | convolution fusion | flops 4718592 | bytes 542728 | tf_op jit(solution)/shard_map/while/body/eval_jaxpr/dot_general | solution.py:161
  46.0 1.8 %fusion.168 = (f32[128]{0:T(128)S(1)}, f32[128]{0:T(128)S(1)}, f32[128]{0:T(128)S(1)}, f32[128]{0:T(128)S(1)}, f32[128]{0:T(128)S(1)}, /*index=5*/f32[128]{0:T(128)S(1)}, f32[1024]{0:T(1024)S(1)}, f32[1024,128]{1,0:T(8,128)S(1)}) fusion(f32[128]{0:T(128)S(1)} %get-tuple-element.387, f32[1024]{0:T(1024)S(1)} %get-tuple-element.388, ...), kind=kOutput, calls=%fused_computation.98.clone.1 | convolution fusion | flops 208828672 | bytes 1600000 | tf_op jit(solution)/shard_map/while/body/eval_jaxpr/dot_general | solution.py:162
  49.2 1.0 %fusion.167 = f32[1024,128]{1,0:T(8,128)S(1)} fusion(f32[1024]{0:T(1024)S(1)} %broadcast_select_fusion.8, f32[128]{0:T(128)S(1)} %get-tuple-element.389, f32[128]{0:T(128)S(1)} %get-tuple-element.387, f32[1024]{0:T(1024)S(1)} %get-tuple-element.388, f32[128]{0:T(128)S(1)} %get-tuple-element.390, f32[128]{0:T(128)S(1)} %get-tuple-element.391, ...), kind=kOutput, calls=%fused_computation.81.clone.1 | convolution fusion | flops 203194368 | bytes 539648 | tf_op jit(solution)/shard_map/while/body/eval_jaxpr/dot_general | solution.py:158
  50.1 1.0 %convolution_bitcast_fusion.4 = f32[1024,128]{1,0:T(8,128)S(1)} fusion(f32[1024,3]{0,1:T(4,128)S(1)} %get-tuple-element.475, f32[4,9,128]{2,1,0:T(8,128)S(1)} %get-tuple-element.474, s32[]{:T(128)} %get-tuple-element.455, s32[]{:T(128)S(6)} %add.997), kind=kOutput, calls=%fused_computation.79.clone.1 | convolution fusion | flops 4718592 | bytes 542728 | tf_op jit(solution)/shard_map/while/body/eval_jaxpr/dot_general | solution.py:161
  51.1 1.8 %fusion.168 = (f32[128]{0:T(128)S(1)}, f32[128]{0:T(128)S(1)}, f32[128]{0:T(128)S(1)}, f32[128]{0:T(128)S(1)}, f32[128]{0:T(128)S(1)}, /*index=5*/f32[128]{0:T(128)S(1)}, f32[1024]{0:T(1024)S(1)}, f32[1024,128]{1,0:T(8,128)S(1)}) fusion(f32[128]{0:T(128)S(1)} %get-tuple-element.387, f32[1024]{0:T(1024)S(1)} %get-tuple-element.388, ...), kind=kOutput, calls=%fused_computation.98.clone.1 | convolution fusion | flops 208828672 | bytes 1600000 | tf_op jit(solution)/shard_map/while/body/eval_jaxpr/dot_general | solution.py:162
  54.2 1.0 %fusion.122 = f32[32,9,128]{2,0,1:T(8,128)} fusion(f32[4,9,128]{2,0,1:T(4,128)S(1)} %get-tuple-element.100, s32[4]{0:T(128)S(1)} %bitcast.139), kind=kOutput, calls=%fused_computation.295 | convolution fusion | flops 1769600 | bytes 165904 | tf_op jit(solution)/shard_map/lr,lkg->rkg/dot_general | solution.py:196
  55.3 17.8 %reduce-scatter.2.cloned.1.call-done = f32[8,9,128]{2,0,1:T(8,128)} async-done(((f32[32,9,128]{2,0,1:T(8,128)}), f32[8,9,128]{2,0,1:T(8,128)}) %reduce-scatter.2.cloned.1.call-update) | async-done | bytes 36880 | tf_op jit(solution)/shard_map/reduce_scatter | solution.py:197
  73.1 0.8 fusion.133
  77.3 1.6 %collective-permute-start.4 = (f32[4,59,128]{2,1,0:T(8,128)S(1)}, f32[4,59,128]{2,1,0:T(8,128)S(1)}, u32[]{:S(2)}, u32[]{:S(2)}) collective-permute-start(f32[4,59,128]{2,1,0:T(8,128)S(1)} %get-tuple-element.277), channel_id=1, source_target_pairs={{0,4},{4,8},{8,12},{12,16},{16,20},{20,24},{24,28},{28,0},{1,5},{5... | collective-permute-start | bytes 362504 | tf_op jit(solution)/shard_map/ppermute | solution.py:36
  79.6 3.0 %collective-permute-done.5 = f32[4,59,128]{2,1,0:T(8,128)S(1)} collective-permute-done((f32[4,59,128]{2,1,0:T(8,128)S(1)}, f32[4,59,128]{2,1,0:T(8,128)S(1)}, u32[]{:S(2)}, u32[]{:S(2)}) %collective-permute-start.5) | collective-permute-done | bytes 120864 | tf_op jit(solution)/shard_map/ppermute | solution.py:36
  83.2 0.8 copy.41
  84.7 0.8 copy.40
  86.2 0.8 copy.39
  (158 shorter events, 19.1 us)
Async XLA Ops:
  7.2 2.3 %copy-start = (f32[8,59,128]{2,0,1:T(8,128)S(1)}, f32[8,59,128]{2,0,1:T(8,128)}, u32[]{:S(2)}) copy-start(f32[8,59,128]{2,0,1:T(8,128)} %param.13) | copy-start | bytes 724996
  7.2 65.9 %reduce-scatter.2.cloned.1.call-start = ((), (), s32[]{:S(2)}) async-start(), calls=%async_computation.1 | async-start | bytes 184320 | tf_op jit(solution)/shard_map/reduce_scatter | solution.py:197
  9.4 0.9 slice-start
  9.5 0.8 copy-start.5
  10.6 5.2 %copy-start.6 = (s32[1,4]{1,0:T(1,128)S(1)}, s32[1,4]{1,0:T(1,128)}, u32[]{:S(2)}) copy-start(s32[1,4]{1,0:T(1,128)} %param.18) | copy-start | bytes 52
  10.6 7.1 %collective-permute-start = (f32[8,9,128]{2,0,1:T(8,128)S(1)}, f32[8,9,128]{2,0,1:T(8,128)S(1)}, u32[]{:S(2)}, u32[]{:S(2)}) collective-permute-start(f32[8,9,128]{2,0,1:T(8,128)S(1)} %constant_dynamic-update-slice_fusion), channel_id=1, source_target_pairs={{0,1},{1,2},{2,3},{3,0},{4,5},{5,6},{6,7},{7,4},{8,9},{9,10},{10,1... | collective-permute-start | bytes 110600 | tf_op jit(solution)/shard_map/ppermute | solution.py:23
  13.7 9.9 %collective-permute-start.2 = (f32[8,9,128]{2,0,1:T(8,128)S(1)}, f32[8,9,128]{2,0,1:T(8,128)S(1)}, u32[]{:S(2)}, u32[]{:S(2)}) collective-permute-start(f32[8,9,128]{2,0,1:T(8,128)S(1)} %constant_dynamic-update-slice_fusion), channel_id=1, source_target_pairs={{0,3},{1,0},{2,1},{3,2},{4,7},{5,4},{6,5},{7,6},{8,11},{9,8},{10,9... | collective-permute-start | bytes 110600 | tf_op jit(solution)/shard_map/ppermute | solution.py:25
  15.8 0.7 copy-start.8
  17.8 5.8 %collective-permute-start.1 = (f32[8,9,128]{2,0,1:T(8,128)S(1)}, f32[8,9,128]{2,0,1:T(8,128)S(1)}, u32[]{:S(2)}, u32[]{:S(2)}) collective-permute-start(f32[8,9,128]{2,0,1:T(8,128)S(1)} %collective-permute-done), channel_id=1, source_target_pairs={{0,1},{1,2},{2,3},{3,0},{4,5},{5,6},{6,7},{7,4},{8,9},{9,10},{10,1... | collective-permute-start | bytes 110600 | tf_op jit(solution)/shard_map/ppermute | solution.py:23
  24.6 9.1 %copy-start.4 = (f32[1,3,1024]{2,0,1:T(1,128)S(1)}, f32[1,3,1024]{2,0,1:T(1,128)}, u32[]{:S(2)}) copy-start(f32[1,3,1024]{2,0,1:T(1,128)} %param.17) | copy-start | bytes 36868
  73.1 0.8 copy-start.3
  74.0 0.9 %copy-start.1 = (f32[8,59,128]{2,0,1:T(8,128)S(1)}, f32[8,59,128]{2,0,1:T(8,128)}, u32[]{:S(2)}) copy-start(f32[8,59,128]{2,0,1:T(8,128)} %param.14) | copy-start | bytes 724996
  74.0 1.1 %copy-start.2 = (f32[8,59,128]{2,0,1:T(8,128)S(1)}, f32[8,59,128]{2,0,1:T(8,128)}, u32[]{:S(2)}) copy-start(f32[8,59,128]{2,0,1:T(8,128)} %param.15) | copy-start | bytes 724996
  74.3 0.8 copy-start.7
  77.2 5.3 %collective-permute-start.5 = (f32[4,59,128]{2,1,0:T(8,128)S(1)}, f32[4,59,128]{2,1,0:T(8,128)S(1)}, u32[]{:S(2)}, u32[]{:S(2)}) collective-permute-start(f32[4,59,128]{2,1,0:T(8,128)S(1)} %get-tuple-element.276), channel_id=1, source_target_pairs={{0,4},{4,8},{8,12},{12,16},{16,20},{20,24},{24,28},{28,0},{1,5},{5... | collective-permute-start | bytes 362504 | tf_op jit(solution)/shard_map/ppermute | solution.py:36
  77.3 6.8 %collective-permute-start.4 = (f32[4,59,128]{2,1,0:T(8,128)S(1)}, f32[4,59,128]{2,1,0:T(8,128)S(1)}, u32[]{:S(2)}, u32[]{:S(2)}) collective-permute-start(f32[4,59,128]{2,1,0:T(8,128)S(1)} %get-tuple-element.277), channel_id=1, source_target_pairs={{0,4},{4,8},{8,12},{12,16},{16,20},{20,24},{24,28},{28,0},{1,5},{5... | collective-permute-start | bytes 362504 | tf_op jit(solution)/shard_map/ppermute | solution.py:36
  78.9 6.7 %collective-permute-start.3 = (f32[4,59,128]{2,1,0:T(8,128)S(1)}, f32[4,59,128]{2,1,0:T(8,128)S(1)}, u32[]{:S(2)}, u32[]{:S(2)}) collective-permute-start(f32[4,59,128]{2,1,0:T(8,128)S(1)} %get-tuple-element.278), channel_id=1, source_target_pairs={{0,4},{4,8},{8,12},{12,16},{16,20},{20,24},{24,28},{28,0},{1,5},{5... | collective-permute-start | bytes 362504 | tf_op jit(solution)/shard_map/ppermute | solution.py:36
Sparse Core Ops, SparseCore 0:
  55.4 17.6 reduce-scatter.1
